TPU v7x, 128 devices: a whole 4x4x4 slice. The times are simulated.
128 devices in a mesh: ctx: 16 (over y_hi, z, core), head: 8 (over x, y_lo).
Axes of the slice: x: 4, y: 4 (y_hi: 2, y_lo: 2; y = y_hi * 2 + y_lo), z: 4, core: 2. Of those that a mesh axis runs over, the one named last changes fastest.
Arguments:
- query_states: bfloat16 [32768, 16, 128], P('ctx', 'head'), may hold values from -36 to 36, as said below
- key_states: bfloat16 [32768, 16, 128], P('ctx', 'head'), may hold values from -6 to 6
- value_states: bfloat16 [32768, 16, 128], P('ctx', 'head'), may hold values from -6 to 6
- block_pattern: int32 [16, 256, 256], P('head'), may hold values 0 or 1
- helper_distances: int32 [2], replicated, may hold values from 1 to 8, as said below
- out_weight: bfloat16 [16, 128, 4096], P('head'), may hold values from -0.125 to 0.125
Outputs:
- layer_output: bfloat16 [32768, 4096], P(('ctx', 'head'))
Inputs may be any that keep to these rules, and one draw needn't show every extreme that they name: `query_states`: Queries; some rows may be large multiples of key rows. `helper_distances`: the two distances differ, and one of them is always 8.
All inputs are finite; a program needn't handle non-finite values. No bound on the sum of `block_pattern` on one device may be relied on, other than what follows from the above.
Results may differ from a plain program's by a relative error of at most 0.015.
Values may be sent and summed in bfloat16 or wider, within the bound.
A program may use at most 128 MiB of HBM per device.

v0:
```python
import jax
import jax.numpy as jnp
from jax import lax
from jax.sharding import PartitionSpec as P

BLOCK = 128


NEG_FILL = -1e30


def as_sent(array):
    return jax.tree.map(lambda a: a.astype(jnp.bfloat16) if a.dtype == jnp.float32 else a, array)


def from_behind(value, axis, steps):
    count = lax.axis_size(axis)
    first, last = (max(0, -steps), min(count, count - steps))
    return lax.ppermute(value, axis, [(source, source + steps) for source in range(first, last)])


def attend_source(query_part, key_part, value_part, pattern_rows, is_local):
    row_count = query_part.shape[0]
    key_count = key_part.shape[0]
    row_step = min(512, row_count)
    score_scale = query_part.shape[2] ** (-0.5)
    key_place = jnp.arange(key_count, dtype=jnp.int32)

    def one_block(block_number):
        first_row = block_number * row_step
        query_rows = lax.dynamic_slice_in_dim(query_part, first_row, row_step, 0)
        pattern_part = lax.dynamic_slice_in_dim(
            pattern_rows, first_row // BLOCK, row_step // BLOCK, 1
        )
        allowed = jnp.repeat(jnp.repeat(pattern_part > 0, BLOCK, axis=1), BLOCK, axis=2)
        if is_local:
            query_place = first_row + jnp.arange(row_step, dtype=jnp.int32)
            query_block = query_place // BLOCK
            key_block = key_place // BLOCK
            earlier = key_block[None, :] < query_block[:, None]
            same_block = (key_block[None, :] == query_block[:, None]) & (
                key_place[None, :] <= query_place[:, None]
            )
            allowed = allowed & earlier[None] | same_block[None]
        scores = (
            jnp.einsum("qhe,khe->hqk", query_rows, key_part, preferred_element_type=jnp.float32)
            * score_scale
        )
        masked = jnp.where(allowed, scores, NEG_FILL)
        row_peak = jnp.max(masked, axis=2)
        weights = jnp.where(allowed, jnp.exp(masked - row_peak[:, :, None]), 0.0)
        row_total = jnp.sum(weights, axis=2)
        numerator = jnp.einsum(
            "hqk,khe->qhe",
            weights.astype(jnp.bfloat16),
            value_part,
            preferred_element_type=jnp.float32,
        )
        return (numerator, row_peak.T, row_total.T)

    numerator, row_peak, row_total = lax.map(
        one_block, jnp.arange(row_count // row_step, dtype=jnp.int32)
    )
    heads_here = query_part.shape[1]
    return (
        numerator.reshape(row_count, heads_here, query_part.shape[2]),
        row_peak.reshape(row_count, heads_here),
        row_total.reshape(row_count, heads_here),
    )


def keep_valid(piece, is_valid):
    numerator, row_peak, row_total = piece
    return (
        jnp.where(is_valid, numerator, 0.0),
        jnp.where(is_valid, row_peak, NEG_FILL),
        jnp.where(is_valid, row_total, 0.0),
    )


def combine_sources(pieces):
    peak_score = pieces[0][1]
    for piece in pieces[1:]:
        peak_score = jnp.maximum(peak_score, piece[1])
    numerator_sum = jnp.zeros_like(pieces[0][0])
    denominator = jnp.zeros_like(pieces[0][1])
    for numerator, row_peak, row_total in pieces:
        factor = jnp.exp(row_peak - peak_score)
        numerator_sum = numerator_sum + factor[:, :, None] * numerator
        denominator = denominator + factor * row_total
    return (numerator_sum / denominator[:, :, None]).astype(jnp.bfloat16)


def bit_on(hop_count, bit_number):
    return hop_count // (1 << bit_number) % 2 == 1


def pick_moved(payload, shifted, hop_counts, bit_number):
    return tuple(
        (
            jnp.where(bit_on(hop_count, bit_number), after, before)
            for before, after, hop_count in zip(payload, shifted, hop_counts)
        )
    )


def send_down(payload, hop_counts):
    levels = lax.axis_size("ctx").bit_length() - 1
    for bit_number in range(levels):
        shifted = jax.tree.map(
            lambda part, own: part.astype(own.dtype),
            from_behind(as_sent(payload), "ctx", -(1 << bit_number)),
            payload,
        )
        payload = pick_moved(payload, shifted, hop_counts, bit_number)
    return payload


def send_up(payload, hop_counts):
    levels = lax.axis_size("ctx").bit_length() - 1
    for bit_number in range(levels):
        shifted = jax.tree.map(
            lambda part, own: part.astype(own.dtype),
            from_behind(as_sent(payload), "ctx", 1 << bit_number),
            payload,
        )
        payload = pick_moved(payload, shifted, hop_counts, bit_number)
    return payload


def pattern_slice(block_pattern, query_shard, key_shard, per_shard):
    starts = (jnp.zeros((), jnp.int32), query_shard * per_shard, key_shard * per_shard)
    return lax.dynamic_slice(block_pattern, starts, (block_pattern.shape[0], per_shard, per_shard))


def per_device(query_states, key_states, value_states, block_pattern, helper_distances, out_weight):
    my_shard = lax.axis_index("ctx")
    shards = lax.axis_size("ctx")
    row_count = query_states.shape[0]
    per_shard = row_count // BLOCK
    pieces = [
        attend_source(
            query_states,
            key_states,
            value_states,
            pattern_slice(block_pattern, my_shard, my_shard, per_shard),
            True,
        )
    ]
    distance_set = (helper_distances[0], helper_distances[1])
    received = [send_down((query_states,), (hop_count,))[0] for hop_count in distance_set]
    answers = []
    for query_in, hop_count in zip(received, distance_set):
        asker = jnp.minimum(my_shard + hop_count, shards - 1)
        answers.append(
            attend_source(
                query_in,
                key_states,
                value_states,
                pattern_slice(block_pattern, asker, my_shard, per_shard),
                False,
            )
        )
    returned = [
        send_up(answer, (hop_count, hop_count, hop_count))
        for answer, hop_count in zip(answers, distance_set)
    ]
    for piece, hop_count in zip(returned, distance_set):
        pieces.append(keep_valid(tuple(piece), my_shard - hop_count >= 0))
    attended = combine_sources(pieces)
    flattened = attended.reshape(row_count, attended.shape[1] * attended.shape[2])
    weight_rows = out_weight.reshape(out_weight.shape[0] * out_weight.shape[1], out_weight.shape[2])
    return lax.psum_scatter(
        jnp.dot(flattened, weight_rows, preferred_element_type=jnp.float32).astype(jnp.bfloat16),
        "head",
        scatter_dimension=0,
        tiled=True,
    )


def solution(mesh):
    placed = (
        P("ctx", "head", None),
        P("ctx", "head", None),
        P("ctx", "head", None),
        P("head", None, None),
        P(),
        P("head", None, None),
    )
    return jax.shard_map(
        per_device, mesh=mesh, in_specs=placed, out_specs=P(("ctx", "head"), None), check_vma=False
    )
```

profile of v0, /device:TPU:23, one launch (start us, length us, event | category | flops | bytes accessed | tf_op | source)
XLA Modules:
  0.0 1023.0 jit_solution(1531431387104549429)
XLA Ops:
  16.1 9.9 collective-permute-done
  28.7 8.7 collective-permute-start.8
  39.9 20.7 %collective-permute-done.8 = bf16[2048,2,128]{2,0,1:T(8,128)(2,1)} collective-permute-done((bf16[2048,2,128]{2,0,1:T(8,128)(2,1)}, bf16[2048,2,128]{2,0,1:T(8,128)(2,1)}, u32[]{:S(2)}, u32[]{:S(2)}) %collective-permute-start.8) | collective-permute-done | bytes 1048608 | tf_op jit(solution)/shard_map/ppermute | solution.py:19
  63.0 3.8 collective-permute-start.9
  67.6 23.5 %collective-permute-done.1 = bf16[2048,2,128]{2,0,1:T(8,128)(2,1)} collective-permute-done((bf16[2048,2,128]{2,0,1:T(8,128)(2,1)}, bf16[2048,2,128]{2,0,1:T(8,128)(2,1)}, u32[]{:S(2)}, u32[]{:S(2)}) %collective-permute-start.1) | collective-permute-done | bytes 1048608 | tf_op jit(solution)/shard_map/ppermute | solution.py:19
  94.2 19.4 %collective-permute-done.9 = bf16[2048,2,128]{2,0,1:T(8,128)(2,1)} collective-permute-done((bf16[2048,2,128]{2,0,1:T(8,128)(2,1)}, bf16[2048,2,128]{2,0,1:T(8,128)(2,1)}, u32[]{:S(2)}, u32[]{:S(2)}) %collective-permute-start.9) | collective-permute-done | bytes 1048608 | tf_op jit(solution)/shard_map/ppermute | solution.py:19
  124.1 12.0 %collective-permute-done.2 = bf16[2048,2,128]{2,0,1:T(8,128)(2,1)} collective-permute-done((bf16[2048,2,128]{2,0,1:T(8,128)(2,1)}, bf16[2048,2,128]{2,0,1:T(8,128)(2,1)}, u32[]{:S(2)}, u32[]{:S(2)}) %collective-permute-start.2) | collective-permute-done | bytes 1048608 | tf_op jit(solution)/shard_map/ppermute | solution.py:19
  140.8 17.8 %collective-permute-done.10 = bf16[2048,2,128]{2,0,1:T(8,128)(2,1)} collective-permute-done((bf16[2048,2,128]{2,0,1:T(8,128)(2,1)}, bf16[2048,2,128]{2,0,1:T(8,128)(2,1)}, u32[]{:S(2)}, u32[]{:S(2)}) %collective-permute-start.10) | collective-permute-done | bytes 1048608 | tf_op jit(solution)/shard_map/ppermute | solution.py:19
  162.4 103.0 %while.52 = (s32[]{:T(128)}, f32[4,512,2,128]{3,1,0,2:T(8,128)}, f32[4,512,2]{1,2,0:T(2,128)S(1)}, f32[4,512,2]{1,2,0:T(2,128)S(1)}, s32[4]{0:T(128)S(1)}, /*ind...) while((s32[]{:T(128)}, f32[4,512,2,128]{3,1,0,2:T(8,128)}, ...), condition=%wide.region_11.12_spmd, body=%wide.region_8.11_spmd.sunk | while | flops 1101002880 | bytes 53282504 | solution.py:61
  163.6 8.4 broadcast_in_dim.275
  172.0 6.6 reshape.254
  178.6 3.6 fusion.121
  189.3 8.4 broadcast_in_dim.275
  197.8 6.6 reshape.254
  204.4 3.6 fusion.121
  215.1 8.4 broadcast_in_dim.275
  223.5 6.6 reshape.254
  230.1 3.6 fusion.121
  240.8 8.4 broadcast_in_dim.275
  249.3 6.6 reshape.254
  255.9 3.6 fusion.121
  271.5 103.0 %while.51 = (s32[]{:T(128)}, f32[4,512,2,128]{3,1,0,2:T(8,128)}, f32[4,512,2]{1,2,0:T(2,128)S(1)}, f32[4,512,2]{1,2,0:T(2,128)S(1)}, s32[4]{0:T(128)S(1)}, /*ind...) while((s32[]{:T(128)}, f32[4,512,2,128]{3,1,0,2:T(8,128)}, ...), condition=%wide.region_7.8_spmd, body=%wide.region_4.7_spmd.sunk | while | flops 1101002880 | bytes 53282504 | solution.py:61
  272.7 8.4 broadcast_in_dim.268
  281.1 6.6 reshape.253
  287.7 3.6 fusion.115
  298.4 8.4 broadcast_in_dim.268
  306.9 6.6 reshape.253
  313.5 3.6 fusion.115
  319.8 3.2 fusion.116
  324.2 8.4 broadcast_in_dim.268
  332.6 6.6 reshape.253
  339.2 3.6 fusion.115
  349.9 8.4 broadcast_in_dim.268
  358.4 6.6 reshape.253
  365.0 3.6 fusion.115
  393.5 20.2 %collective-permute-done.12 = bf16[2048,2]{0,1:T(2,128)(2,1)S(1)} collective-permute-done((bf16[2048,2]{0,1:T(2,128)(2,1)S(1)}, bf16[2048,2]{0,1:T(2,128)(2,1)S(1)}, u32[]{:S(2)}, u32[]{:S(2)}) %collective-permute-start.12) | collective-permute-done | bytes 8224 | tf_op jit(solution)/shard_map/ppermute | solution.py:19
  434.9 31.6 %collective-permute-done.16 = bf16[2048,2,128]{2,0,1:T(8,128)(2,1)S(1)} collective-permute-done((bf16[2048,2,128]{2,0,1:T(8,128)(2,1)S(1)}, bf16[2048,2,128]{2,0,1:T(8,128)(2,1)S(1)}, u32[]{:S(2)}, u32[]{:S(2)}) %collective-permute-start.16) | collective-permute-done | bytes 1048608 | tf_op jit(solution)/shard_map/ppermute | solution.py:19
  471.7 20.2 %collective-permute-done.20 = bf16[2048,2,128]{2,0,1:T(8,128)(2,1)S(1)} collective-permute-done((bf16[2048,2,128]{2,0,1:T(8,128)(2,1)S(1)}, bf16[2048,2,128]{2,0,1:T(8,128)(2,1)S(1)}, u32[]{:S(2)}, u32[]{:S(2)}) %collective-permute-start.20) | collective-permute-done | bytes 1048608 | tf_op jit(solution)/shard_map/ppermute | solution.py:19
  497.2 5.6 collective-permute-done.17
  507.2 18.7 %collective-permute-done.21 = bf16[2048,2,128]{2,0,1:T(8,128)(2,1)S(1)} collective-permute-done((bf16[2048,2,128]{2,0,1:T(8,128)(2,1)S(1)}, bf16[2048,2,128]{2,0,1:T(8,128)(2,1)S(1)}, u32[]{:S(2)}, u32[]{:S(2)}) %collective-permute-start.21) | collective-permute-done | bytes 1048608 | tf_op jit(solution)/shard_map/ppermute | solution.py:19
  533.4 131.1 %while.53 = (s32[]{:T(128)}, f32[4,512,2,128]{3,1,0,2:T(8,128)}, f32[4,512,2]{1,2,0:T(2,128)S(1)}, f32[4,512,2]{1,2,0:T(2,128)S(1)}, s32[4]{0:T(128)S(1)}, /*ind...) while((s32[]{:T(128)}, f32[4,512,2,128]{3,1,0,2:T(8,128)}, ...), condition=%wide.region_3.4_spmd.clone.clone, body=%wide.region_0.3_spmd.clone.clone.sunk | while | flops 1117805184 | bytes 57505460 | solution.py:61
  534.7 8.5 broadcast_in_dim.282
  543.2 6.6 reshape.255
  552.1 4.0 fusion.127
  556.1 4.2 fusion.129
  560.3 5.8 fusion.128
  567.5 8.5 broadcast_in_dim.282
  575.9 6.6 reshape.255
  584.9 4.0 fusion.127
  588.9 4.2 fusion.129
  593.1 5.8 fusion.128
  600.2 8.5 broadcast_in_dim.282
  608.7 6.6 reshape.255
  617.6 4.0 fusion.127
  621.7 4.2 fusion.129
  625.9 5.8 fusion.128
  633.0 8.5 broadcast_in_dim.282
  641.5 6.6 reshape.255
  650.4 4.0 fusion.127
  654.4 4.2 fusion.129
  658.6 5.8 fusion.128
  665.9 7.2 fusion.66
  673.1 8.1 bitcast_convert_fusion
  681.2 334.9 %reduce-scatter.2.cloned.1.call-done = bf16[256,4096]{1,0:T(8,128)(2,1)} async-done(((bf16[2048,4096]{1,0:T(8,128)(2,1)}), bf16[256,4096]{1,0:T(8,128)(2,1)}) %reduce-scatter.2.cloned.1.call-update) | async-done | bytes 2097168 | tf_op jit(solution)/shard_map/reduce_scatter | solution.py:173
  (243 shorter events, 162.3 us)
Async XLA Ops:
  6.5 666.6 %copy-start = (bf16[2,128,4096]{2,1,0:T(8,128)(2,1)S(1)}, bf16[2,128,4096]{2,1,0:T(8,128)(2,1)}, u32[]{:S(2)}) copy-start(bf16[2,128,4096]{2,1,0:T(8,128)(2,1)} %param.17) | copy-start | bytes 6291460
  6.5 19.4 %copy-start.8 = (bf16[2048,2,128]{2,1,0:T(2,128)(2,1)S(1)}, bf16[2048,2,128]{2,1,0:T(2,128)(2,1)}, u32[]{:S(2)}) copy-start(bf16[2048,2,128]{2,1,0:T(2,128)(2,1)} %param.12) | copy-start | bytes 3145732
  6.5 5.1 copy-start.14
  6.5 1009.6 %reduce-scatter.2.cloned.1.call-start = ((), (), s32[]{:S(2)}) async-start(), calls=%async_computation.1 | async-start | bytes 18874368 | tf_op jit(solution)/shard_map/reduce_scatter | solution.py:173
  9.0 16.9 %collective-permute-start = (bf16[2048,2,128]{2,0,1:T(8,128)(2,1)}, bf16[2048,2,128]{2,0,1:T(8,128)(2,1)}, u32[]{:S(2)}, u32[]{:S(2)}) collective-permute-start(bf16[2048,2,128]{2,0,1:T(8,128)(2,1)} %copy.18), channel_id=1, source_target_pairs={{8,0},{16,8},{24,16},{32,24},{40,32},{48,40},{56,48},{64,56},{72,6... | collective-permute-start | bytes 3145736 | tf_op jit(solution)/shard_map/ppermute | solution.py:19
  28.7 62.4 %copy-start.9 = (bf16[2048,2,128]{2,0,1:T(8,128)(2,1)S(1)}, bf16[2048,2,128]{2,0,1:T(8,128)(2,1)}, u32[]{:S(2)}) copy-start(bf16[2048,2,128]{2,0,1:T(8,128)(2,1)} %get-tuple-element.624) | copy-start | bytes 3145732
  28.7 32.0 %collective-permute-start.8 = (bf16[2048,2,128]{2,0,1:T(8,128)(2,1)}, bf16[2048,2,128]{2,0,1:T(8,128)(2,1)}, u32[]{:S(2)}, u32[]{:S(2)}) collective-permute-start(bf16[2048,2,128]{2,0,1:T(8,128)(2,1)} %get-tuple-element.625), channel_id=1, source_target_pairs={{16,0},{24,8},{32,16},{40,24},{48,32},{56,40},{64,48},{72,56},{80,... | collective-permute-start | bytes 3145736 | tf_op jit(solution)/shard_map/ppermute | solution.py:19
  38.0 53.1 %collective-permute-start.1 = (bf16[2048,2,128]{2,0,1:T(8,128)(2,1)}, bf16[2048,2,128]{2,0,1:T(8,128)(2,1)}, u32[]{:S(2)}, u32[]{:S(2)}) collective-permute-start(bf16[2048,2,128]{2,0,1:T(8,128)(2,1)} %get-tuple-element.624), channel_id=1, source_target_pairs={{16,0},{24,8},{32,16},{40,24},{48,32},{56,40},{64,48},{72,56},{80,... | collective-permute-start | bytes 3145736 | tf_op jit(solution)/shard_map/ppermute | solution.py:19
  63.0 50.6 %collective-permute-start.9 = (bf16[2048,2,128]{2,0,1:T(8,128)(2,1)}, bf16[2048,2,128]{2,0,1:T(8,128)(2,1)}, u32[]{:S(2)}, u32[]{:S(2)}) collective-permute-start(bf16[2048,2,128]{2,0,1:T(8,128)(2,1)} %broadcast_select_fusion.1), channel_id=1, source_target_pairs={{32,0},{40,8},{48,16},{56,24},{64,32},{72,40},{80,48},{88,56},{96,... | collective-permute-start | bytes 3145736 | tf_op jit(solution)/shard_map/ppermute | solution.py:19
  92.3 43.8 %collective-permute-start.2 = (bf16[2048,2,128]{2,0,1:T(8,128)(2,1)}, bf16[2048,2,128]{2,0,1:T(8,128)(2,1)}, u32[]{:S(2)}, u32[]{:S(2)}) collective-permute-start(bf16[2048,2,128]{2,0,1:T(8,128)(2,1)} %broadcast_select_fusion.5), channel_id=1, source_target_pairs={{32,0},{40,8},{48,16},{56,24},{64,32},{72,40},{80,48},{88,56},{96,... | collective-permute-start | bytes 3145736 | tf_op jit(solution)/shard_map/ppermute | solution.py:19
  115.9 42.6 %collective-permute-start.10 = (bf16[2048,2,128]{2,0,1:T(8,128)(2,1)}, bf16[2048,2,128]{2,0,1:T(8,128)(2,1)}, u32[]{:S(2)}, u32[]{:S(2)}) collective-permute-start(bf16[2048,2,128]{2,0,1:T(8,128)(2,1)} %broadcast_select_fusion.2), channel_id=1, source_target_pairs={{64,0},{72,8},{80,16},{88,24},{96,32},{104,40},{112,48},{120,56},{... | collective-permute-start | bytes 3145736 | tf_op jit(solution)/shard_map/ppermute | solution.py:19
  138.5 129.0 %collective-permute-start.3 = (bf16[2048,2,128]{2,0,1:T(8,128)(2,1)}, bf16[2048,2,128]{2,0,1:T(8,128)(2,1)}, u32[]{:S(2)}, u32[]{:S(2)}) collective-permute-start(bf16[2048,2,128]{2,0,1:T(8,128)(2,1)} %broadcast_select_fusion.6), channel_id=1, source_target_pairs={{64,0},{72,8},{80,16},{88,24},{96,32},{104,40},{112,48},{120,56},{... | collective-permute-start | bytes 3145736 | tf_op jit(solution)/shard_map/ppermute | solution.py:19
  178.6 3.6 copy-start.1
  182.3 2.7 copy-start.12
  204.4 3.6 copy-start.1
  208.0 2.7 copy-start.12
  230.1 3.6 copy-start.1
  233.8 2.7 copy-start.12
  255.8 3.6 copy-start.1
  259.5 2.7 copy-start.12
  265.4 120.3 %collective-permute-start.11 = (bf16[2048,2]{0,1:T(2,128)(2,1)S(1)}, bf16[2048,2]{0,1:T(2,128)(2,1)S(1)}, u32[]{:S(2)}, u32[]{:S(2)}) collective-permute-start(bf16[2048,2]{0,1:T(2,128)(2,1)S(1)} %convert_element_type.177), channel_id=1, source_target_pairs={{0,8},{8,16},{16,24},{24,32},{32,40},{40,48},{48,56},{56,64},{64,7... | collective-permute-start | bytes 24584 | tf_op jit(solution)/shard_map/ppermute | solution.py:19
  287.7 3.6 copy-start.2
  291.4 2.7 copy-start.13
  313.4 3.6 copy-start.2
  317.1 2.7 copy-start.13
  339.2 3.6 copy-start.2
  342.9 2.7 copy-start.13
  364.9 3.6 copy-start.2
  368.6 2.7 copy-start.13
  374.5 13.2 %collective-permute-start.4 = (bf16[2048,2]{0,1:T(2,128)(2,1)S(1)}, bf16[2048,2]{0,1:T(2,128)(2,1)S(1)}, u32[]{:S(2)}, u32[]{:S(2)}) collective-permute-start(bf16[2048,2]{0,1:T(2,128)(2,1)S(1)} %convert_element_type.169), channel_id=1, source_target_pairs={{0,8},{8,16},{16,24},{24,32},{32,40},{40,48},{48,56},{56,64},{64,7... | collective-permute-start | bytes 24584 | tf_op jit(solution)/shard_map/ppermute | solution.py:19
  376.4 13.2 %collective-permute-start.23 = (bf16[2048,2]{0,1:T(2,128)(2,1)S(1)}, bf16[2048,2]{0,1:T(2,128)(2,1)S(1)}, u32[]{:S(2)}, u32[]{:S(2)}) collective-permute-start(bf16[2048,2]{0,1:T(2,128)(2,1)S(1)} %convert_element_type.201), channel_id=1, source_target_pairs={{0,8},{8,16},{16,24},{24,32},{32,40},{40,48},{48,56},{56,64},{64,7... | collective-permute-start | bytes 24584 | tf_op jit(solution)/shard_map/ppermute | solution.py:19
  378.4 13.2 %collective-permute-start.27 = (bf16[2048,2]{0,1:T(2,128)(2,1)S(1)}, bf16[2048,2]{0,1:T(2,128)(2,1)S(1)}, u32[]{:S(2)}, u32[]{:S(2)}) collective-permute-start(bf16[2048,2]{0,1:T(2,128)(2,1)S(1)} %convert_element_type.209), channel_id=1, source_target_pairs={{0,8},{8,16},{16,24},{24,32},{32,40},{40,48},{48,56},{56,64},{64,7... | collective-permute-start | bytes 24584 | tf_op jit(solution)/shard_map/ppermute | solution.py:19
  382.0 42.0 %collective-permute-start.15 = (bf16[2048,2,128]{2,0,1:T(8,128)(2,1)S(1)}, bf16[2048,2,128]{2,0,1:T(8,128)(2,1)S(1)}, u32[]{:S(2)}, u32[]{:S(2)}) collective-permute-start(bf16[2048,2,128]{2,0,1:T(8,128)(2,1)S(1)} %bitcast_convert_fusion.2), channel_id=1, source_target_pairs={{0,8},{8,16},{16,24},{24,32},{32,40},{40,48},{48,56},{56,64},{64,7... | collective-permute-start | bytes 3145736 | tf_op jit(solution)/shard_map/ppermute | solution.py:19
  385.7 44.1 %collective-permute-start.19 = (bf16[2048,2,128]{2,0,1:T(8,128)(2,1)S(1)}, bf16[2048,2,128]{2,0,1:T(8,128)(2,1)S(1)}, u32[]{:S(2)}, u32[]{:S(2)}) collective-permute-start(bf16[2048,2,128]{2,0,1:T(8,128)(2,1)S(1)} %bitcast_convert_fusion.1), channel_id=1, source_target_pairs={{0,8},{8,16},{16,24},{24,32},{32,40},{40,48},{48,56},{56,64},{64,7... | collective-permute-start | bytes 3145736 | tf_op jit(solution)/shard_map/ppermute | solution.py:19
  387.7 26.1 %collective-permute-start.12 = (bf16[2048,2]{0,1:T(2,128)(2,1)S(1)}, bf16[2048,2]{0,1:T(2,128)(2,1)S(1)}, u32[]{:S(2)}, u32[]{:S(2)}) collective-permute-start(bf16[2048,2]{0,1:T(2,128)(2,1)S(1)} %fusion.75), channel_id=1, source_target_pairs={{0,16},{8,24},{16,32},{24,40},{32,48},{40,56},{48,64},{56,72},{64,... | collective-permute-start | bytes 24584 | tf_op jit(solution)/shard_map/ppermute | solution.py:19
  389.6 26.1 %collective-permute-start.5 = (bf16[2048,2]{0,1:T(2,128)(2,1)S(1)}, bf16[2048,2]{0,1:T(2,128)(2,1)S(1)}, u32[]{:S(2)}, u32[]{:S(2)}) collective-permute-start(bf16[2048,2]{0,1:T(2,128)(2,1)S(1)} %fusion.73), channel_id=1, source_target_pairs={{0,16},{8,24},{16,32},{24,40},{32,48},{40,56},{48,64},{56,72},{64,... | collective-permute-start | bytes 24584 | tf_op jit(solution)/shard_map/ppermute | solution.py:19
  391.6 26.1 %collective-permute-start.24 = (bf16[2048,2]{0,1:T(2,128)(2,1)S(1)}, bf16[2048,2]{0,1:T(2,128)(2,1)S(1)}, u32[]{:S(2)}, u32[]{:S(2)}) collective-permute-start(bf16[2048,2]{0,1:T(2,128)(2,1)S(1)} %fusion.77), channel_id=1, source_target_pairs={{0,16},{8,24},{16,32},{24,40},{32,48},{40,56},{48,64},{56,72},{64,... | collective-permute-start | bytes 24584 | tf_op jit(solution)/shard_map/ppermute | solution.py:19
  413.7 8.4 collective-permute-start.28
  415.7 12.1 %collective-permute-start.13 = (bf16[2048,2]{0,1:T(2,128)(2,1)S(1)}, bf16[2048,2]{0,1:T(2,128)(2,1)S(1)}, u32[]{:S(2)}, u32[]{:S(2)}) collective-permute-start(bf16[2048,2]{0,1:T(2,128)(2,1)S(1)} %get-tuple-element.606), channel_id=1, source_target_pairs={{0,32},{8,40},{16,48},{24,56},{32,64},{40,72},{48,80},{56,88},{64,... | collective-permute-start | bytes 24584 | tf_op jit(solution)/shard_map/ppermute | solution.py:19
  417.7 15.2 %collective-permute-start.6 = (bf16[2048,2]{0,1:T(2,128)(2,1)S(1)}, bf16[2048,2]{0,1:T(2,128)(2,1)S(1)}, u32[]{:S(2)}, u32[]{:S(2)}) collective-permute-start(bf16[2048,2]{0,1:T(2,128)(2,1)S(1)} %get-tuple-element.608), channel_id=1, source_target_pairs={{0,32},{8,40},{16,48},{24,56},{32,64},{40,72},{48,80},{56,88},{64,... | collective-permute-start | bytes 24584 | tf_op jit(solution)/shard_map/ppermute | solution.py:19
  422.1 47.6 %collective-permute-start.25 = (bf16[2048,2]{0,1:T(2,128)(2,1)S(1)}, bf16[2048,2]{0,1:T(2,128)(2,1)S(1)}, u32[]{:S(2)}, u32[]{:S(2)}) collective-permute-start(bf16[2048,2]{0,1:T(2,128)(2,1)S(1)} %get-tuple-element.602), channel_id=1, source_target_pairs={{0,32},{8,40},{16,48},{24,56},{32,64},{40,72},{48,80},{56,88},{64,... | collective-permute-start | bytes 24584 | tf_op jit(solution)/shard_map/ppermute | solution.py:19
  424.1 80.0 %copy-start.4 = (bf16[2048,2,128]{2,0,1:T(8,128)(2,1)}, bf16[2048,2,128]{2,0,1:T(8,128)(2,1)S(1)}, u32[]{:S(2)}) copy-start(bf16[2048,2,128]{2,0,1:T(8,128)(2,1)S(1)} %collective-permute-done.15) | copy-start | bytes 3145732
  424.1 71.1 %collective-permute-start.29 = (bf16[2048,2]{0,1:T(2,128)(2,1)S(1)}, bf16[2048,2]{0,1:T(2,128)(2,1)S(1)}, u32[]{:S(2)}, u32[]{:S(2)}) collective-permute-start(bf16[2048,2]{0,1:T(2,128)(2,1)S(1)} %get-tuple-element.604), channel_id=1, source_target_pairs={{0,32},{8,40},{16,48},{24,56},{32,64},{40,72},{48,80},{56,88},{64,... | collective-permute-start | bytes 24584 | tf_op jit(solution)/shard_map/ppermute | solution.py:19
  427.8 38.6 %collective-permute-start.16 = (bf16[2048,2,128]{2,0,1:T(8,128)(2,1)S(1)}, bf16[2048,2,128]{2,0,1:T(8,128)(2,1)S(1)}, u32[]{:S(2)}, u32[]{:S(2)}) collective-permute-start(bf16[2048,2,128]{2,0,1:T(8,128)(2,1)S(1)} %fusion.71), channel_id=1, source_target_pairs={{0,16},{8,24},{16,32},{24,40},{32,48},{40,56},{48,64},{56,72},{64,... | collective-permute-start | bytes 3145736 | tf_op jit(solution)/shard_map/ppermute | solution.py:19
  429.8 97.4 %copy-start.5 = (bf16[2048,2,128]{2,0,1:T(8,128)(2,1)}, bf16[2048,2,128]{2,0,1:T(8,128)(2,1)S(1)}, u32[]{:S(2)}) copy-start(bf16[2048,2,128]{2,0,1:T(8,128)(2,1)S(1)} %collective-permute-done.19) | copy-start | bytes 3145732
  429.8 100.6 %collective-permute-start.14 = (bf16[2048,2]{0,1:T(2,128)(2,1)S(1)}, bf16[2048,2]{0,1:T(2,128)(2,1)S(1)}, u32[]{:S(2)}, u32[]{:S(2)}) collective-permute-start(bf16[2048,2]{0,1:T(2,128)(2,1)S(1)} %fusion.76), channel_id=1, source_target_pairs={{0,64},{8,72},{16,80},{24,88},{32,96},{40,104},{48,112},{56,120},{... | collective-permute-start | bytes 24584 | tf_op jit(solution)/shard_map/ppermute | solution.py:19
  432.9 59.0 %collective-permute-start.20 = (bf16[2048,2,128]{2,0,1:T(8,128)(2,1)S(1)}, bf16[2048,2,128]{2,0,1:T(8,128)(2,1)S(1)}, u32[]{:S(2)}, u32[]{:S(2)}) collective-permute-start(bf16[2048,2,128]{2,0,1:T(8,128)(2,1)S(1)} %fusion.72), channel_id=1, source_target_pairs={{0,16},{8,24},{16,32},{24,40},{32,48},{40,56},{48,64},{56,72},{64,... | collective-permute-start | bytes 3145736 | tf_op jit(solution)/shard_map/ppermute | solution.py:19
  466.5 37.6 %copy-start.6 = (bf16[2048,2,128]{2,0,1:T(8,128)(2,1)}, bf16[2048,2,128]{2,0,1:T(8,128)(2,1)S(1)}, u32[]{:S(2)}) copy-start(bf16[2048,2,128]{2,0,1:T(8,128)(2,1)S(1)} %collective-permute-done.16) | copy-start | bytes 3145732
  466.5 199.2 %collective-permute-start.7 = (bf16[2048,2]{0,1:T(2,128)(2,1)S(1)}, bf16[2048,2]{0,1:T(2,128)(2,1)S(1)}, u32[]{:S(2)}, u32[]{:S(2)}) collective-permute-start(bf16[2048,2]{0,1:T(2,128)(2,1)S(1)} %fusion.74), channel_id=1, source_target_pairs={{0,64},{8,72},{16,80},{24,88},{32,96},{40,104},{48,112},{56,120},{... | collective-permute-start | bytes 24584 | tf_op jit(solution)/shard_map/ppermute | solution.py:19
  469.8 33.0 %collective-permute-start.17 = (bf16[2048,2,128]{2,0,1:T(8,128)(2,1)S(1)}, bf16[2048,2,128]{2,0,1:T(8,128)(2,1)S(1)}, u32[]{:S(2)}, u32[]{:S(2)}) collective-permute-start(bf16[2048,2,128]{2,0,1:T(8,128)(2,1)S(1)} %fusion.67), channel_id=1, source_target_pairs={{0,32},{8,40},{16,48},{24,56},{32,64},{40,72},{48,80},{56,88},{64,... | collective-permute-start | bytes 3145736 | tf_op jit(solution)/shard_map/ppermute | solution.py:19
  491.9 35.3 %copy-start.7 = (bf16[2048,2,128]{2,0,1:T(8,128)(2,1)}, bf16[2048,2,128]{2,0,1:T(8,128)(2,1)S(1)}, u32[]{:S(2)}) copy-start(bf16[2048,2,128]{2,0,1:T(8,128)(2,1)S(1)} %collective-permute-done.20) | copy-start | bytes 3145732
  491.9 173.8 %collective-permute-start.26 = (bf16[2048,2]{0,1:T(2,128)(2,1)S(1)}, bf16[2048,2]{0,1:T(2,128)(2,1)S(1)}, u32[]{:S(2)}, u32[]{:S(2)}) collective-permute-start(bf16[2048,2]{0,1:T(2,128)(2,1)S(1)} %fusion.78), channel_id=1, source_target_pairs={{0,64},{8,72},{16,80},{24,88},{32,96},{40,104},{48,112},{56,120},{... | collective-permute-start | bytes 24584 | tf_op jit(solution)/shard_map/ppermute | solution.py:19
  495.2 30.7 %collective-permute-start.21 = (bf16[2048,2,128]{2,0,1:T(8,128)(2,1)S(1)}, bf16[2048,2,128]{2,0,1:T(8,128)(2,1)S(1)}, u32[]{:S(2)}, u32[]{:S(2)}) collective-permute-start(bf16[2048,2,128]{2,0,1:T(8,128)(2,1)S(1)} %fusion.68), channel_id=1, source_target_pairs={{0,32},{8,40},{16,48},{24,56},{32,64},{40,72},{48,80},{56,88},{64,... | collective-permute-start | bytes 3145736 | tf_op jit(solution)/shard_map/ppermute | solution.py:19
  502.8 4.5 copy-start.10
  502.8 163.0 %collective-permute-start.30 = (bf16[2048,2]{0,1:T(2,128)(2,1)S(1)}, bf16[2048,2]{0,1:T(2,128)(2,1)S(1)}, u32[]{:S(2)}, u32[]{:S(2)}) collective-permute-start(bf16[2048,2]{0,1:T(2,128)(2,1)S(1)} %fusion.80), channel_id=1, source_target_pairs={{0,64},{8,72},{16,80},{24,88},{32,96},{40,104},{48,112},{56,120},{... | collective-permute-start | bytes 24584 | tf_op jit(solution)/shard_map/ppermute | solution.py:19
  525.9 4.5 copy-start.11
  525.9 139.9 %collective-permute-start.18 = (bf16[2048,2,128]{2,0,1:T(8,128)(2,1)}, bf16[2048,2,128]{2,0,1:T(8,128)(2,1)}, u32[]{:S(2)}, u32[]{:S(2)}) collective-permute-start(bf16[2048,2,128]{2,0,1:T(8,128)(2,1)} %fusion.69), channel_id=1, source_target_pairs={{0,64},{8,72},{16,80},{24,88},{32,96},{40,104},{48,112},{56,120},{... | collective-permute-start | bytes 3145736 | tf_op jit(solution)/shard_map/ppermute | solution.py:19
  530.4 135.5 %collective-permute-start.22 = (bf16[2048,2,128]{2,0,1:T(8,128)(2,1)}, bf16[2048,2,128]{2,0,1:T(8,128)(2,1)}, u32[]{:S(2)}, u32[]{:S(2)}) collective-permute-start(bf16[2048,2,128]{2,0,1:T(8,128)(2,1)} %fusion.70), channel_id=1, source_target_pairs={{0,64},{8,72},{16,80},{24,88},{32,96},{40,104},{48,112},{56,120},{... | collective-permute-start | bytes 3145736 | tf_op jit(solution)/shard_map/ppermute | solution.py:19
  549.8 2.3 copy-start.3
  582.5 2.3 copy-start.3
  615.3 2.3 copy-start.3
  648.0 2.3 copy-start.3
Sparse Core Ops, SparseCore 0:
  681.4 334.7 reduce-scatter.1
where the time goes:
time: 1030 us; the launch traced here: 1020 us
  waiting for transfers between devices  537 us (52%)
  local copies, waits for them, and re-layouts  200 us (19%)
  matrix products  102 us (10%)
  other arithmetic  88.4 us (9%)
  starting transfers between devices  66.1 us (6%)
  between operations  21.8 us (2%)
    reduce_scatter x1, waiting for transfers between devices, per_device(): lax.psum_scatter(jnp.dot(flattened, weight_rows, preferred_element_type=j...  335 us
    ppermute x31, waiting for transfers between devices, from_behind(): lax.ppermute(value, axis, [(source, source + steps) for source in range(f...  202 us
    broadcast_in_dim x12, local copies, waits for them, and re-layouts, one_block(): jnp.repeat(jnp.repeat(pattern_part > 0, BLOCK, axis=1), BLOCK, axis=2)  101 us
    reshape x12, local copies, waits for them, and re-layouts, one_block(): jnp.repeat(jnp.repeat(pattern_part > 0, BLOCK, axis=1), BLOCK, axis=2)  78.9 us
    ppermute x31, starting transfers between devices, from_behind(): lax.ppermute(value, axis, [(source, source + steps) for source in range(f...  66.1 us
    dot_general x12, matrix products, one_block(): jnp.einsum('hqk,khe->qhe', weights.astype(jnp.bfloat16), value_part, pref...  48.5 us
    dot_general x12, matrix products, one_block(): jnp.einsum('qhe,khe->hqk', query_rows, key_part, preferred_element_type=j...  45.2 us
    reduce_sum x12, other arithmetic, one_block(): row_total = jnp.sum(weights, axis=2)  38.3 us
  transfers between devices with their start and end apart: 32, of which 13 were waited for; matrix products, arithmetic and copies ran while one was open for 36% of the time, Pallas kernels for 0%

commit v1 on v0

v1 whole, which is shorter than its diff:
```python
import functools

import jax
import jax.numpy as jnp
from jax import lax
from jax.experimental import pallas as pl
from jax.experimental.pallas import tpu as pltpu
from jax.sharding import PartitionSpec as P

BLOCK = 128
HEAD_DIM = 128
NEG = -1e30
BIG = 1e30
SCALE = HEAD_DIM**-0.5 * 1.4426950408889634
FAR = 8
TILE = 256
PAIR = 2 * TILE
STAT_ROWS = 16
OUT_ROWS = HEAD_DIM + STAT_ROWS
BF16 = jnp.bfloat16
F32 = jnp.float32
NT = (((1,), (1,)), ((), ()))
NN = (((1,), (0,)), ((), ()))
MESH = pl.DeviceIdType.MESH
WHOLE = pl.BlockSpec(memory_space=pltpu.VMEM)
VMEM_LIMIT = 60 << 20


def three_parts(x):
    first = x.astype(BF16)
    rest = x - first.astype(F32)
    second = rest.astype(BF16)
    return [first.astype(F32), second.astype(F32), rest - second.astype(F32)]


def aligned(value, factor):
    return pl.multiple_of(value * factor, factor)


def whole_kernel(
    near, shards, places,
    pattern, q_raw, k_raw, v_raw, w_own, out_ref,
    wide, keys, values, queries, made, came, s_a, s_b, diag_a, diag_b, peak_ref,
    peak_start, acc_start, total_start, att_out, att_in, w_all,
    q_sent, q_came, made_sent, made_came, att_sent, att_came, w_sent, w_came,
):
    shard = lax.axis_index("ctx")
    place = lax.axis_index("head")
    core = lax.rem(shard, 2)
    x, y = place // 2, lax.rem(place, 2)
    xs = places // 2
    beside = 2 * x + 1 - y
    up = 2 * lax.rem(x + 1, xs) + y
    down = 2 * lax.rem(x + xs - 1, xs) + y
    twin = shard + 1 - 2 * core
    rows = keys.shape[1]
    blocks = rows // BLOCK
    chunks = rows // TILE
    tiles = rows // TILE
    slots = 6
    reach = (FAR, near)
    asked = [shard + r < shards for r in reach]
    helped = [shard >= r for r in reach]

    def to_ctx(index):
        return {"ctx": index}

    def to_head(index):
        return {"head": index}

    def remote(src, dst, sent, landed, device):
        return pltpu.make_async_remote_copy(
            src_ref=src, dst_ref=dst, send_sem=sent, recv_sem=landed,
            device_id=device, device_id_type=MESH,
        )

    barrier = pltpu.get_barrier_semaphore()
    pl.semaphore_signal(barrier, inc=1, device_id=to_ctx(twin), device_id_type=MESH)

    def greet(n, carry):
        other = lax.rem(place + n, places)
        pl.semaphore_signal(barrier, inc=1, device_id=to_head(other), device_id_type=MESH)
        return carry

    lax.fori_loop(1, places, greet, 0)
    for r, has, gets in zip(reach, asked, helped):
        @pl.when(has)
        def _():
            pl.semaphore_signal(barrier, inc=1, device_id=to_ctx(shard + r), device_id_type=MESH)

        @pl.when(gets)
        def _():
            pl.semaphore_signal(barrier, inc=1, device_id=to_ctx(shard - r), device_id_type=MESH)

    def split_queries(i, carry):
        wide[0] = q_raw[pl.ds(aligned(i, PAIR), PAIR), :].astype(F32)
        for h in range(2):
            queries[h, pl.ds(aligned(i, TILE), TILE), :] = wide[
                0, pl.ds(h, TILE, stride=2), :
            ].astype(BF16)
        return carry

    lax.fori_loop(0, tiles, split_queries, 0)
    peers = [jnp.where(flag, 1, 0) for flag in asked + helped]
    pl.semaphore_wait(barrier, places + peers[0] + peers[1] + peers[2] + peers[3])

    def query_copy(h, source):
        n = 2 * h + source
        return remote(
            queries.at[h], queries.at[2 + n], q_sent.at[n], q_came.at[n],
            to_ctx(jnp.where(helped[source], shard - reach[source], shard + reach[source])),
        )

    columns = w_own.shape[2] // 2
    mine = pl.ds(aligned(core, columns), columns)

    def weight_copy(n, device, slot, source=None, part=None):
        head = slice(None) if part is None else part
        src = (w_own if source is None else w_all.at[slot]).at[head, :, mine]
        return remote(src, w_all.at[slot, head, :, mine], w_sent.at[n], w_came.at[n], device)

    across = 2 * lax.rem(x + 2, xs) + y
    across_beside = 2 * lax.rem(x + 2, xs) + 1 - y
    up_beside = 2 * lax.rem(x + 1, xs) + 1 - y
    down_beside = 2 * lax.rem(x + xs - 1, xs) + 1 - y
    sends = {
        0: lambda: weight_copy(0, to_head(beside), place),
        1: lambda: weight_copy(1, to_head(up), place),
        2: lambda: weight_copy(2, to_head(down), place),
        3: lambda: weight_copy(3, to_head(up), down, True, 1),
        4: lambda: weight_copy(4, to_head(down), up, True, 0),
        5: lambda: weight_copy(5, to_head(up), beside, True),
        6: lambda: weight_copy(6, to_head(down), beside, True),
        7: lambda: weight_copy(7, to_head(beside), across, True),
    }
    origins = {
        0: (beside, None), 1: (down, None), 2: (up, None), 3: (across, 1), 4: (across, 0),
        5: (down_beside, None), 6: (up_beside, None), 7: (across_beside, None),
    }
    swaps = {8: beside, 9: down, 10: up, 11: across, 12: down_beside, 13: up_beside, 14: across_beside}

    def swap_copy(n):
        return weight_copy(n, to_ctx(twin), swaps[n], True)

    def weight_wait(n):
        slot, part = origins[n]
        weight_copy(n, to_head(beside), slot, True, part).wait_recv()

    for h in range(2):
        for source in range(2):
            @pl.when(helped[source])
            def _():
                query_copy(h, source).start()
        if h == 0:
            for n in range(3):
                sends[n]().start()

    def split_kv(i, carry):
        wide[0] = k_raw[pl.ds(aligned(i, PAIR), PAIR), :].astype(F32)
        wide[1] = v_raw[pl.ds(aligned(i, PAIR), PAIR), :].astype(F32)
        for h in range(2):
            to = pl.ds(aligned(i, TILE), TILE)
            keys[h, to, :] = wide[0, pl.ds(h, TILE, stride=2), :].astype(BF16)
            values[h, :, to] = wide[1, pl.ds(h, TILE, stride=2), :].T.astype(BF16)
        return carry

    lax.fori_loop(0, tiles, split_kv, 0)

    def where_of(t):
        slot, u = t // tiles, lax.rem(t, tiles)
        h = jnp.where(slot < 2, slot, (slot - 2) // 2)
        return slot, u, h

    def flags(slot, u, i):
        limit = jnp.where(slot < 2, 2 * u, blocks)
        parts = []
        for b in range(2):
            bit = pattern[(slot * blocks + 2 * u + b) * blocks + i]
            bit = jnp.where(i < limit + b, bit, 0)
            parts.append(jnp.full((8, BLOCK), bit, jnp.int32))
        return jnp.concatenate(parts, 1) > 0

    place_k = lax.broadcasted_iota(jnp.int32, (TILE, TILE), 0)
    place_q = lax.broadcasted_iota(jnp.int32, (TILE, TILE), 1)

    def phase(t1, t2, first, second, odd):
        s_first, diag_first = first
        s_second, diag_second = second
        slot2, u2, h2 = where_of(t2)
        peak2 = peak_ref[...]
        if t1 is not None:
            slot1, u1, h1 = where_of(t1)
            q = queries[slot1, pl.ds(aligned(u1, TILE), TILE), :]

            @pl.when(t2 < 2 * tiles)
            def _():
                here = pl.ds(aligned(u1, TILE), TILE)
                s = lax.dot_general(keys[h1, here, :], q, NT, preferred_element_type=F32)
                same = (place_k // BLOCK) == (place_q // BLOCK)
                s = jnp.where(same & (place_k <= place_q) & (slot1 < 2), s, NEG)
                diag_first[...] = s
                peak_start[...] = s.reshape(TILE // 8, 8, TILE).max(0)
                p = jnp.exp2((diag_second[...].reshape(TILE // 8, 8, TILE) - peak2) * SCALE)
                total_start[...] = p.sum(0)
                there = pl.ds(aligned(u2, TILE), TILE)
                acc_start[...] = lax.dot_general(
                    values[h2, :, there], p.reshape(TILE, TILE).astype(BF16), NN,
                    preferred_element_type=F32,
                )

            @pl.when(t2 == 2 * tiles)
            def _():
                peak_start[...] = jnp.full_like(peak_start, NEG)
                total_start[...] = jnp.zeros_like(total_start)
                acc_start[...] = jnp.zeros_like(acc_start)

            peak1 = peak_start[...]
        total = total_start[...]
        acc = acc_start[...]
        for j in range(chunks):
            chunk = slice(j * TILE, (j + 1) * TILE)
            if t1 is not None:
                s = lax.dot_general(keys[h1, chunk, :], q, NT, preferred_element_type=F32)
                s_first[chunk] = s
                for b in range(2):
                    block_peak = s[b * BLOCK : (b + 1) * BLOCK].reshape(BLOCK // 8, 8, TILE).max(0)
                    allowed = flags(slot1, u1, 2 * j + b)
                    peak1 = jnp.maximum(peak1, jnp.where(allowed, block_peak, NEG))
            parts = []
            for b in range(2):
                i = 2 * j + b
                shift = jnp.where(flags(slot2, u2, i), peak2, BIG)
                s2 = s_second[i * BLOCK : (i + 1) * BLOCK].reshape(BLOCK // 8, 8, TILE)
                p = jnp.exp2((s2 - shift) * SCALE)
                total = total + p.sum(0)
                parts.append(p.reshape(BLOCK, TILE).astype(BF16))
            acc = acc + lax.dot_general(
                values[h2, :, chunk], jnp.concatenate(parts, 0), NN, preferred_element_type=F32
            )
        total = total.sum(0, keepdims=True)
        inverse = jnp.where(total > 0, 1.0 / jnp.where(total > 0, total, 1.0), 0.0)
        stats = three_parts(peak2[0:1]) + three_parts(total)
        stats.append(jnp.zeros((STAT_ROWS - 6, TILE), F32))
        made[t2 // 2, :, odd * TILE : (odd + 1) * TILE] = jnp.concatenate(
            [acc * inverse] + stats, 0
        ).astype(BF16)
        if t1 is not None:
            peak_ref[...] = jnp.broadcast_to(peak1.max(0, keepdims=True), (8, TILE))

    pairs = tiles // 2
    own_pairs = 2 * pairs

    def answer_copy(pair, source):
        n = pair - own_pairs
        return remote(
            made.at[pair], came.at[n], made_sent.at[n], made_came.at[n],
            to_ctx(jnp.where(asked[source], shard + reach[source], shard - reach[source])),
        )

    def send_answer(pair):
        for source in range(2):
            @pl.when((pair >= own_pairs) & (lax.rem(pair // pairs, 2) == source) & asked[source])
            def _():
                answer_copy(pair, source).start()

    def merge_pair(h, n):
        answers = [2 * h * pairs + n, (2 * h + 1) * pairs + n]
        for source in range(2):
            @pl.when(helped[source])
            def _():
                answer_copy(own_pairs + answers[source], source).wait_recv()
        for half in range(2):
            lanes = slice(half * TILE, (half + 1) * TILE)
            pieces = []
            for r in range(3):
                part = (made[h * pairs + n, :, lanes] if r == 0 else came[answers[r - 1], :, lanes])
                part = part.astype(F32)
                if r > 0:
                    part = jnp.where(helped[r - 1], part, 0.0)
                stats = part[HEAD_DIM : HEAD_DIM + 8]
                peak = stats[0:1] + stats[1:2] + stats[2:3]
                total = stats[3:4] + stats[4:5] + stats[5:6]
                if r > 0:
                    peak = jnp.where(helped[r - 1], peak, NEG)
                pieces.append((part[:HEAD_DIM], peak, total))
            top = jnp.maximum(jnp.maximum(pieces[0][1], pieces[1][1]), pieces[2][1])
            factors = [jnp.exp2((peak - top) * SCALE) * total for _, peak, total in pieces]
            inverse = 1.0 / (factors[0] + factors[1] + factors[2])
            mixed = sum(part * (factor * inverse) for (part, _, _), factor in zip(pieces, factors))
            att_out[h, 2 * n + half] = mixed.T.astype(BF16)

    def att_copy(h, u):
        return remote(
            att_out.at[h, u], att_in.at[place, h], att_sent.at[h, u], att_came.at[h, place],
            to_head(u),
        )

    def send_rows(h, n):
        for half in range(2):
            u = 2 * n + half

            @pl.when(u == place)
            def _():
                att_in[place, h] = att_out[h, u]

            @pl.when(u != place)
            def _():
                att_copy(h, u).start()

    peak_ref[...] = jnp.zeros_like(peak_ref)
    diag_b[...] = jnp.full_like(diag_b, NEG)
    a, b = (s_a, diag_a), (s_b, diag_b)
    steps = slots * tiles // 2

    def step(i, carry):
        for n in range(4):
            @pl.when((i == own_pairs + n * pairs) & asked[n % 2])
            def _():
                query_copy(n // 2, n % 2).wait_recv()

        @pl.when(i == own_pairs + 4)
        def _():
            for n in (1, 2):
                weight_wait(n)
            for n in (3, 4):
                sends[n]().start()
            weight_wait(0)
            for n in (5, 6):
                sends[n]().start()
            for n in (8, 9, 10):
                swap_copy(n).start()

        @pl.when(i == own_pairs + 12)
        def _():
            for n in (3, 4):
                weight_wait(n)
            sends[7]().start()
            swap_copy(11).start()

        phase(2 * i, jnp.maximum(2 * i - 1, 0), a, b, 1)
        phase(2 * i + 1, 2 * i, b, a, 0)
        send_answer(i - 1)

        late = i - (steps - pairs)

        @pl.when(late >= 1)
        def _():
            send_rows(0, late - 1)

        @pl.when(late >= 0)
        def _():
            merge_pair(0, late)

        return carry

    lax.fori_loop(0, steps, step, 0)
    phase(None, slots * tiles - 1, a, b, 1)
    send_rows(0, pairs - 1)
    send_answer(steps - 1)

    def merge_rest(n, carry):
        @pl.when(n < pairs)
        def _():
            merge_pair(1, n)

        @pl.when(n >= 1)
        def _():
            send_rows(1, n - 1)

        return carry

    lax.fori_loop(0, pairs + 1, merge_rest, 0)
    for n in (5, 6):
        weight_wait(n)
    for n in (12, 13):
        swap_copy(n).start()
    weight_wait(7)
    swap_copy(14).start()
    for n in swaps:
        swap_wait = weight_copy(n, to_ctx(twin), swaps[n], True)
        other = pl.ds(aligned(1 - core, columns), columns)
        remote(
            w_all.at[swaps[n], :, :, other], w_all.at[swaps[n], :, :, other],
            w_sent.at[n], w_came.at[n], to_ctx(twin),
        ).wait_recv()
        swap_wait.wait_send()
    for n in range(8):
        sends[n]().wait_send()

    def rows_wait(n, carry):
        g = lax.rem(place + n, places)
        for h in range(2):
            remote(
                att_out.at[h, g], att_in.at[g, h], att_sent.at[h, g], att_came.at[h, g], to_head(g)
            ).wait()
        return carry

    lax.fori_loop(1, places, rows_wait, 0)

    width = 256

    def project(c, carry):
        cols = pl.ds(aligned(c, width), width)
        acc = None
        for n in range(places):
            g = lax.rem(place + n, places)
            left = jnp.concatenate([att_in[g, 0], att_in[g, 1]], 1)
            right = (w_own[:, :, cols] if n == 0 else w_all[g, :, :, cols]).reshape(
                2 * HEAD_DIM, width
            )
            term = lax.dot_general(left, right, NN, preferred_element_type=F32)
            acc = term if acc is None else acc + term
        out_ref[:, cols] = acc.astype(BF16)
        return carry

    lax.fori_loop(0, out_ref.shape[1] // width, project, 0)

    for source in range(2):
        @pl.when(helped[source])
        def _():
            for h in range(2):
                query_copy(h, source).wait_send()

        @pl.when(asked[source])
        def _():
            for h in range(2):
                for n in range(pairs):
                    answer_copy(own_pairs + (2 * h + source) * pairs + n, source).wait_send()


def planned(near, shards, places, pattern, q, k, v, w):
    rows = q.shape[0]
    flat = lambda array: array.reshape(rows * 2, HEAD_DIM)
    tiles = rows // TILE
    pairs = tiles // 2
    answers = 4 * pairs
    dma = pltpu.SemaphoreType.DMA
    vm = pltpu.VMEM
    return pl.pallas_call(
        functools.partial(whole_kernel, near, shards, places),
        in_specs=[pl.BlockSpec(memory_space=pltpu.SMEM)] + [WHOLE] * 4,
        out_specs=WHOLE,
        out_shape=jax.ShapeDtypeStruct((rows // places, w.shape[2]), BF16),
        scratch_shapes=[
            vm((2, PAIR, HEAD_DIM), F32),
            vm((2, rows, HEAD_DIM), BF16),
            vm((2, HEAD_DIM, rows), BF16),
            vm((6, rows, HEAD_DIM), BF16),
            vm((2 * pairs + answers, OUT_ROWS, PAIR), BF16),
            vm((answers, OUT_ROWS, PAIR), BF16),
            vm((rows, TILE), F32),
            vm((rows, TILE), F32),
            vm((TILE, TILE), F32),
            vm((TILE, TILE), F32),
            vm((8, TILE), F32),
            vm((8, TILE), F32),
            vm((HEAD_DIM, TILE), F32),
            vm((8, TILE), F32),
            vm((2, places, TILE, HEAD_DIM), BF16),
            vm((places, 2, TILE, HEAD_DIM), BF16),
            vm((places, 2, HEAD_DIM, w.shape[2]), BF16),
            dma((4,)), dma((4,)), dma((answers,)), dma((answers,)),
            dma((2, places)), dma((2, places)), dma((15,)), dma((15,)),
        ],
        compiler_params=pltpu.CompilerParams(
            collective_id=near, has_side_effects=True, vmem_limit_bytes=VMEM_LIMIT
        ),
        name=f"whole_{near}",
    )(pattern, flat(q), flat(k), flat(v), w)


def per_device(query_states, key_states, value_states, block_pattern, helper_distances, out_weight):
    shard = lax.axis_index("ctx")
    shards = lax.axis_size("ctx")
    places = lax.axis_size("head")
    near = jnp.minimum(helper_distances[0], helper_distances[1])
    blocks = query_states.shape[0] // BLOCK

    def bits(distance):
        asker = jnp.minimum(shard + distance, shards - 1)
        starts = (jnp.zeros((), jnp.int32), asker * blocks, shard * blocks)
        return lax.dynamic_slice(block_pattern, starts, (2, blocks, blocks))

    own, far, close = bits(0), bits(FAR), bits(near)
    pattern = jnp.concatenate([own, far[:1], close[:1], far[1:], close[1:]]).reshape(-1)
    branches = [functools.partial(planned, r, shards, places) for r in range(1, FAR)]
    return lax.switch(
        near - 1, branches, pattern, query_states, key_states, value_states, out_weight
    )


def solution(mesh):
    placed = (
        P("ctx", "head", None),
        P("ctx", "head", None),
        P("ctx", "head", None),
        P("head", None, None),
        P(),
        P("head", None, None),
    )
    return jax.shard_map(
        per_device, mesh=mesh, in_specs=placed, out_specs=P(("ctx", "head"), None), check_vma=False
    )
```

time: 1030 us -> 155 us (0.15)
  waiting for transfers between devices: 537 us -> 0 us
  local copies, waits for them, and re-layouts: 200 us -> 7.21 us
  Pallas kernels: 0 us -> 144 us
  matrix products: 102 us -> 0 us
  other arithmetic: 88.4 us -> 0 us
  starting transfers between devices: 66.1 us -> 0 us
  between operations: 21.8 us -> 1.31 us
    reduce_scatter x1 -> x0, waiting for transfers between devices: 335 us -> none  [per_device(): lax.psum_scatter(jnp.dot(flattened, weight_rows, preferred_element_type=j...]
    ppermute x31 -> x0, waiting for transfers between devices: 202 us -> none  [from_behind(): lax.ppermute(value, axis, [(source, source + steps) for source in range(f...]
    pallas_call x0 -> x1, Pallas kernels: none -> 144 us  [planned(): pl.pallas_call(functools.partial(whole_kernel, near, shards, places), in_...]
    dot_general x25 -> x0, matrix products: 102 us -> none  [the longest x12 48.5 us: one_block(): jnp.einsum('hqk,khe->qhe', weights.astype(jnp.bfloat16), value_part, pref...]
    broadcast_in_dim x24 -> x0, local copies, waits for them, and re-layouts: 102 us -> none  [the longest x12 101 us: one_block(): jnp.repeat(jnp.repeat(pattern_part > 0, BLOCK, axis=1), BLOCK, axis=2)]
    reshape x12 -> x1, local copies, waits for them, and re-layouts: 78.9 us -> 0.68 us  [per_device(): jnp.concatenate([own, far[:1], close[:1], far[1:], close[1:]]).reshape(-1)]
    ppermute x31 -> x0, starting transfers between devices: 66.1 us -> none  [from_behind(): lax.ppermute(value, axis, [(source, source + steps) for source in range(f...]
    reduce_sum x12 -> x0, other arithmetic: 38.3 us -> none  [one_block(): row_total = jnp.sum(weights, axis=2)]
  transfers between devices with their start and end apart: 32 -> 0, of which waited for: 13 -> 0; matrix products, arithmetic and copies ran while one was open for 36% -> 0% of each run, Pallas kernels for 0% -> 0%
where the time goes in v1:
time: 155 us; the launch traced here: 153 us
  Pallas kernels  144 us (93%)
  local copies, waits for them, and re-layouts  7.21 us (5%)
    pallas_call x1, Pallas kernels, planned(): pl.pallas_call(functools.partial(whole_kernel, near, shards, places), in_...  144 us
    unnamed x5, local copies, waits for them, and re-layouts  4.44 us

profile of v1, /device:TPU:23, one launch (start us, length us, event | category | flops | bytes accessed | tf_op | source)
XLA Modules:
  0.0 153.3 jit_solution(11974318859531250032)
XLA Ops:
  0.0 1.3 fusion
  2.6 0.8 dynamic-slice_dynamic-update-slice_fusion
  3.4 0.8 constant_dynamic-update-slice_fusion.3
  4.2 0.8 constant_dynamic-update-slice_fusion.2
  5.0 0.8 constant_dynamic-update-slice_fusion.1
  5.7 0.8 constant_dynamic-update-slice_fusion
  6.5 145.5 %conditional.1 = (bf16[256,4096]{1,0:T(8,128)(2,1)S(1)}) conditional(s32[]{:T(128)} %clamp.3, (bf16[2048,2,128]{2,1,0:T(2,128)(2,1)}, bf16[2048,2,128]{2,1,0:T(2,128)(2,1)}, bf16[2048,2,128]{2,1,0:T(2,128)(2,1)}, s32[6,16,16]{2,1,0:T(8,128)S(1)}, bf16[2,128,4096]{2,1,0:T(8,128)(2,1)}) %tuple.26, ...), branch_computations={%region_0.0_spmd, %region_1.0_spmd, %region_2.0_spmd, %region_3.0_... | conditional | bytes 12296 | solution.py:487
  6.5 0.7 reshape.72.pattern
  7.2 144.3 %whole_5.1 = bf16[256,4096]{1,0:T(8,128)(2,1)S(1)} custom-call(s32[1536]{0:T(1024)} %reshape.72.pattern, bf16[4096,128]{1,0:T(8,128)(2,1)} %bitcast.26, bf16[4096,128]{1,0:T(8,128)(2,1)} %bitcast.33, bf16[4096,128]{1,0:T(8,128)(2,1)} %bitcast.40, bf16[2,128,4096]{2,1,0:T(8,128)(2,1)} %get-tuple-element.179.w_own), custom_call_target="tpu_custom_call" | custom-call | tf_op jit(solution)/shard_map/cond/branch_4_fun/whole_5/pallas_call | solution.py:439
  152.0 1.3 copy.54

commit v2 on v1

v2 whole, which is shorter than its diff:
```python
import functools

import jax
import jax.numpy as jnp
from jax import lax
from jax.experimental import pallas as pl
from jax.experimental.pallas import tpu as pltpu
from jax.sharding import PartitionSpec as P

BLOCK = 128
HEAD_DIM = 128
NEG = -1e30
BIG = 1e30
SCALE = HEAD_DIM**-0.5 * 1.4426950408889634
FAR = 8
TILE = 256
PAIR = 2 * TILE
STAT_ROWS = 16
OUT_ROWS = HEAD_DIM + STAT_ROWS
BF16 = jnp.bfloat16
F32 = jnp.float32
NT = (((1,), (1,)), ((), ()))
NN = (((1,), (0,)), ((), ()))
MESH = pl.DeviceIdType.MESH
WHOLE = pl.BlockSpec(memory_space=pltpu.VMEM)
VMEM_LIMIT = 60 << 20
LAG = 3
EVENTS = (10, 13, 16, 23)


def three_parts(x):
    first = x.astype(BF16)
    rest = x - first.astype(F32)
    second = rest.astype(BF16)
    return [first.astype(F32), second.astype(F32), rest - second.astype(F32)]


def aligned(value, factor):
    return pl.multiple_of(value * factor, factor)


def whole_kernel(
    near, shards, places,
    pattern_all, q_raw, k_raw, v_raw, w_own, out_ref,
    pattern, wide, keys, values, queries, made, came, s_a, s_b, diag_a, diag_b, peak_ref,
    peak_start, acc_start, total_start, att_out, att_in, w_all,
    q_sent, q_came, made_sent, made_came, att_sent, att_came, w_sent, w_came, spread_sent, spread_came, bits_came,
):
    shard = lax.axis_index("ctx")
    place = lax.axis_index("head")
    core = lax.rem(shard, 2)
    x, y = place // 2, lax.rem(place, 2)
    xs = places // 2
    beside = 2 * x + 1 - y
    up = 2 * lax.rem(x + 1, xs) + y
    down = 2 * lax.rem(x + xs - 1, xs) + y
    twin = shard + 1 - 2 * core
    z = lax.rem(shard // 2, 4)
    odd_z = lax.rem(z, 2)
    z_up = shard + 2 * lax.rem(z + 1, 4) - 2 * z
    z_down = shard + 2 * lax.rem(z + 3, 4) - 2 * z
    rows = keys.shape[1]
    blocks = rows // BLOCK
    chunks = rows // TILE
    tiles = rows // TILE
    pairs = tiles // 2
    groups = 2 * pairs
    reach = (FAR, near)
    asked = [shard + r < shards for r in reach]
    helped = [shard >= r for r in reach]

    def to_ctx(index):
        return {"ctx": index}

    def to_head(index):
        return {"head": index}

    def remote(src, dst, sent, landed, device):
        return pltpu.make_async_remote_copy(
            src_ref=src, dst_ref=dst, send_sem=sent, recv_sem=landed,
            device_id=device, device_id_type=MESH,
        )

    def bits_copy(source):
        asker = shard if source == 0 else jnp.minimum(shard + reach[source - 1], shards - 1)
        return pltpu.make_async_copy(
            pattern_all.at[:, pl.ds(aligned(asker, blocks), blocks), :],
            pattern.at[source],
            bits_came.at[source],
        )

    for source in range(3):
        bits_copy(source).start()

    barrier = pltpu.get_barrier_semaphore()
    for other in (twin, z_up, z_down):
        pl.semaphore_signal(barrier, inc=1, device_id=to_ctx(other), device_id_type=MESH)

    def greet(n, carry):
        other = lax.rem(place + n, places)
        pl.semaphore_signal(barrier, inc=1, device_id=to_head(other), device_id_type=MESH)
        return carry

    lax.fori_loop(1, places, greet, 0)
    for r, has, gets in zip(reach, asked, helped):
        @pl.when(has)
        def _():
            pl.semaphore_signal(barrier, inc=1, device_id=to_ctx(shard + r), device_id_type=MESH)

        @pl.when(gets)
        def _():
            pl.semaphore_signal(barrier, inc=1, device_id=to_ctx(shard - r), device_id_type=MESH)

    def split_queries(i, carry):
        wide[0] = q_raw[pl.ds(aligned(i, PAIR), PAIR), :].astype(F32)
        for h in range(2):
            queries[h, pl.ds(aligned(i, TILE), TILE), :] = wide[
                0, pl.ds(h, TILE, stride=2), :
            ].astype(BF16)
        return carry

    lax.fori_loop(0, tiles, split_queries, 0)
    peers = [jnp.where(flag, 1, 0) for flag in asked + helped]
    pl.semaphore_wait(barrier, places + 2 + peers[0] + peers[1] + peers[2] + peers[3])

    def query_copy(n, source):
        h, rows_here = n // pairs, pl.ds(aligned(lax.rem(n, pairs), PAIR), PAIR)
        sem = source * groups + n
        return remote(
            queries.at[h, rows_here], queries.at[2 + 2 * h + source, rows_here],
            q_sent.at[sem], q_came.at[sem],
            to_ctx(jnp.where(helped[source], shard - reach[source], shard + reach[source])),
        )

    def send_queries(n, carry):
        for source in range(2):
            @pl.when(helped[source])
            def _():
                query_copy(n, source).start()

        return carry

    columns = w_own.shape[2] // 2
    share = columns * 3 // 16
    direct = pl.ds(aligned(core * 16 + odd_z * 6, columns // 16), columns * 5 // 8)
    lacking = pl.ds(aligned(core * 16 + (1 - odd_z) * 10, columns // 16), 2 * share)

    def block(parity, second):
        return pl.ds(aligned(core * 16 + parity * 10 + second * 3, columns // 16), share)

    def weight_copy(n, device, slot, cols, source=None, part=None, sent=None, came=None):
        head = slice(None) if part is None else part
        src = (w_own if source is None else w_all.at[slot]).at[head, :, cols]
        sent, came = (w_sent if sent is None else sent), (w_came if came is None else came)
        return remote(src, w_all.at[slot, head, :, cols], sent.at[n], came.at[n], device)

    def slot_of(p):
        p = jnp.asarray(p, jnp.int32)
        side = jnp.where((p == 0) | (p >= 4), 1 - y, y)
        kind = lax.rem(p, 3)
        hop = jnp.where(p == 0, 0, jnp.where(kind == 1, xs - 1, jnp.where(kind == 2, 1, 2)))
        return 2 * lax.rem(x + hop, xs) + side

    routes = [
        (beside, None, None), (up, None, None), (down, None, None),
        (up, 1, 1), (down, 2, 0), (up, 0, None), (down, 0, None), (up, 4, 1), (down, 5, 0),
    ]
    arrivals = [(0, None), (1, None), (2, None), (3, 1), (3, 0), (4, None), (5, None), (6, 1), (6, 0)]

    def forward(n):
        device, piece, part = routes[n]
        slot = place if piece is None else slot_of(piece)
        return weight_copy(n, to_head(device), slot, direct, piece, part)

    def arrived(n):
        piece, part = arrivals[n]
        weight_copy(n, to_head(beside), slot_of(piece), direct, True, part).wait_recv()

    def spread_copy(p, kind):
        device = (z_down, z_up, twin, twin)[kind]
        cols = (block(odd_z, 0), block(odd_z, 1), direct, lacking)[kind]
        return weight_copy(
            4 * p + kind, to_ctx(device), slot_of(p), cols, True, None, spread_sent, spread_came
        )

    def spread_wait(p, kind):
        theirs = (1 - core) * 16
        cols = (
            block(1 - odd_z, 0), block(1 - odd_z, 1),
            pl.ds(aligned(theirs + odd_z * 6, columns // 16), columns * 5 // 8),
            pl.ds(aligned(theirs + (1 - odd_z) * 10, columns // 16), 2 * share),
        )[kind]
        device = (z_up, z_down, twin, twin)[kind]
        weight_copy(
            4 * p + kind, to_ctx(device), slot_of(p), cols, True, None, spread_sent, spread_came
        ).wait_recv()

    def spread(first, last):
        def body(p, carry):
            for kind in range(3):
                spread_copy(p, kind).start()
            return carry

        lax.fori_loop(first, last + 1, body, 0)

    def settle(first, last):
        def body(p, carry):
            for kind in range(2):
                spread_wait(p, kind)
            spread_copy(p, 3).start()
            return carry

        lax.fori_loop(first, last + 1, body, 0)

    lax.fori_loop(0, pairs, send_queries, 0)
    for n in range(3):
        forward(n).start()
    lax.fori_loop(pairs, groups, send_queries, 0)

    def split_kv(i, carry):
        wide[0] = k_raw[pl.ds(aligned(i, PAIR), PAIR), :].astype(F32)
        wide[1] = v_raw[pl.ds(aligned(i, PAIR), PAIR), :].astype(F32)
        for h in range(2):
            to = pl.ds(aligned(i, TILE), TILE)
            keys[h, to, :] = wide[0, pl.ds(h, TILE, stride=2), :].astype(BF16)
            values[h, :, to] = wide[1, pl.ds(h, TILE, stride=2), :].T.astype(BF16)
        return carry

    lax.fori_loop(0, tiles, split_kv, 0)

    def where_of(t):
        pair = t // 2
        kind, n = lax.rem(pair, 3), pair // 3
        h = n // pairs
        u = 2 * lax.rem(n, pairs) + lax.rem(t, 2)
        slot = jnp.where(kind == 0, h, 1 + 2 * h + kind)
        return kind, slot, u, h, kind * groups + n

    def flags(kind, h, u, i):
        limit = jnp.where(kind == 0, 2 * u, blocks)
        parts = []
        for b in range(2):
            bit = pattern[kind, h, 2 * u + b, shard * blocks + i]
            bit = jnp.where(i < limit + b, bit, 0)
            parts.append(jnp.full((8, BLOCK), bit, jnp.int32))
        return jnp.concatenate(parts, 1) > 0

    place_k = lax.broadcasted_iota(jnp.int32, (TILE, TILE), 0)
    place_q = lax.broadcasted_iota(jnp.int32, (TILE, TILE), 1)

    def phase(t1, t2, first, second, odd):
        s_first, diag_first = first
        s_second, diag_second = second
        kind2, slot2, u2, h2, made2 = where_of(t2)
        peak2 = peak_ref[...]
        if t1 is not None:
            kind1, slot1, u1, h1, made1 = where_of(t1)
            q = queries[slot1, pl.ds(aligned(u1, TILE), TILE), :]

            @pl.when((kind1 == 0) | (kind2 == 0))
            def _():
                here = pl.ds(aligned(u1, TILE), TILE)
                s = lax.dot_general(keys[h1, here, :], q, NT, preferred_element_type=F32)
                same = (place_k // BLOCK) == (place_q // BLOCK)
                s = jnp.where(same & (place_k <= place_q) & (kind1 == 0), s, NEG)
                diag_first[...] = s
                peak_start[...] = s.reshape(TILE // 8, 8, TILE).max(0)
                shift = jnp.where(kind2 == 0, peak2, BIG)
                p = jnp.exp2((diag_second[...].reshape(TILE // 8, 8, TILE) - shift) * SCALE)
                total_start[...] = p.sum(0)
                there = pl.ds(aligned(u2, TILE), TILE)
                acc_start[...] = lax.dot_general(
                    values[h2, :, there], p.reshape(TILE, TILE).astype(BF16), NN,
                    preferred_element_type=F32,
                )

            @pl.when((kind1 != 0) & (kind2 != 0))
            def _():
                peak_start[...] = jnp.full_like(peak_start, NEG)
                total_start[...] = jnp.zeros_like(total_start)
                acc_start[...] = jnp.zeros_like(acc_start)

            peak1 = peak_start[...]
        total = total_start[...]
        acc = acc_start[...]
        for j in range(chunks):
            chunk = slice(j * TILE, (j + 1) * TILE)
            if t1 is not None:
                s = lax.dot_general(keys[h1, chunk, :], q, NT, preferred_element_type=F32)
                s_first[chunk] = s
                for b in range(2):
                    block_peak = s[b * BLOCK : (b + 1) * BLOCK].reshape(BLOCK // 8, 8, TILE).max(0)
                    allowed = flags(kind1, h1, u1, 2 * j + b)
                    peak1 = jnp.maximum(peak1, jnp.where(allowed, block_peak, NEG))
            parts = []
            for b in range(2):
                i = 2 * j + b
                shift = jnp.where(flags(kind2, h2, u2, i), peak2, BIG)
                s2 = s_second[i * BLOCK : (i + 1) * BLOCK].reshape(BLOCK // 8, 8, TILE)
                p = jnp.exp2((s2 - shift) * SCALE)
                total = total + p.sum(0)
                parts.append(p.reshape(BLOCK, TILE).astype(BF16))
            acc = acc + lax.dot_general(
                values[h2, :, chunk], jnp.concatenate(parts, 0), NN, preferred_element_type=F32
            )
        total = total.sum(0, keepdims=True)
        inverse = jnp.where(total > 0, 1.0 / jnp.where(total > 0, total, 1.0), 0.0)
        stats = three_parts(peak2[0:1]) + three_parts(total)
        stats.append(jnp.zeros((STAT_ROWS - 6, TILE), F32))
        made[made2, :, odd * TILE : (odd + 1) * TILE] = jnp.concatenate(
            [acc * inverse] + stats, 0
        ).astype(BF16)
        if t1 is not None:
            peak_ref[...] = jnp.broadcast_to(peak1.max(0, keepdims=True), (8, TILE))

    def answer_copy(n, source):
        sem = source * groups + n
        return remote(
            made.at[(1 + source) * groups + n], came.at[sem], made_sent.at[sem], made_came.at[sem],
            to_ctx(jnp.where(asked[source], shard + reach[source], shard - reach[source])),
        )

    def send_answer(i):
        for source in range(2):
            @pl.when((i >= 0) & (lax.rem(i + 3, 3) == 1 + source) & asked[source])
            def _():
                answer_copy(i // 3, source).start()

    def merge_pair(n):
        h = n // pairs
        for source in range(2):
            @pl.when(helped[source])
            def _():
                answer_copy(n, source).wait_recv()
        for half in range(2):
            lanes = slice(half * TILE, (half + 1) * TILE)
            pieces = []
            for r in range(3):
                part = made[n, :, lanes] if r == 0 else came[(r - 1) * groups + n, :, lanes]
                part = part.astype(F32)
                if r > 0:
                    part = jnp.where(helped[r - 1], part, 0.0)
                stats = part[HEAD_DIM : HEAD_DIM + 8]
                peak = stats[0:1] + stats[1:2] + stats[2:3]
                total = stats[3:4] + stats[4:5] + stats[5:6]
                if r > 0:
                    peak = jnp.where(helped[r - 1], peak, NEG)
                pieces.append((part[:HEAD_DIM], peak, total))
            top = jnp.maximum(jnp.maximum(pieces[0][1], pieces[1][1]), pieces[2][1])
            factors = [jnp.exp2((peak - top) * SCALE) * total for _, peak, total in pieces]
            inverse = 1.0 / (factors[0] + factors[1] + factors[2])
            mixed = sum(part * (factor * inverse) for (part, _, _), factor in zip(pieces, factors))
            att_out[h, 2 * lax.rem(n, pairs) + half] = mixed.T.astype(BF16)

    def att_copy(h, u):
        return remote(
            att_out.at[h, u], att_in.at[place, h], att_sent.at[h, u], att_came.at[h, place],
            to_head(u),
        )

    def send_rows(n):
        h = n // pairs
        for half in range(2):
            u = 2 * lax.rem(n, pairs) + half

            @pl.when(u == place)
            def _():
                att_in[place, h] = att_out[h, u]

            @pl.when(u != place)
            def _():
                att_copy(h, u).start()

    def combine(n):
        @pl.when((n >= 1) & (n <= groups))
        def _():
            send_rows(n - 1)

        @pl.when((n >= 0) & (n < groups))
        def _():
            merge_pair(n)

    peak_ref[...] = jnp.zeros_like(peak_ref)
    diag_a[...] = jnp.full_like(diag_a, NEG)
    diag_b[...] = jnp.full_like(diag_b, NEG)
    a, b = (s_a, diag_a), (s_b, diag_b)
    steps = 3 * groups
    lag = LAG
    for source in range(3):
        bits_copy(source).wait()

    def step(i, carry):
        for source in range(2):
            @pl.when((lax.rem(i, 3) == 1 + source) & asked[source])
            def _():
                query_copy(i // 3, source).wait_recv()

        @pl.when(i == EVENTS[0])
        def _():
            for n in (1, 2):
                arrived(n)
            for n in (3, 4):
                forward(n).start()
            spread(1, 2)

        @pl.when(i == EVENTS[1])
        def _():
            arrived(0)
            for n in (5, 6):
                forward(n).start()
            spread(0, 0)

        @pl.when(i == EVENTS[2])
        def _():
            for n in (3, 4):
                arrived(n)
            spread(3, 3)
            settle(1, 2)

        @pl.when(i == EVENTS[3])
        def _():
            for n in (5, 6):
                arrived(n)
            for n in (7, 8):
                forward(n).start()
            spread(4, 5)
            settle(0, 0)

        phase(2 * i, jnp.maximum(2 * i - 1, 0), a, b, 1)
        phase(2 * i + 1, 2 * i, b, a, 0)
        send_answer(i - 1)

        @pl.when(lax.rem(i, 3) == 0)
        def _():
            combine(i // 3 - lag)

        return carry

    lax.fori_loop(0, steps, step, 0)
    phase(None, 2 * steps - 1, a, b, 1)
    send_answer(steps - 1)

    def merge_rest(n, carry):
        combine(n)
        return carry

    lax.fori_loop(groups - lag, groups + 1, merge_rest, 0)
    for n in (7, 8):
        arrived(n)
    spread(6, 6)
    settle(3, 6)
    for n in range(9):
        forward(n).wait_send()

    def spread_end(p, carry):
        for kind in (2, 3):
            spread_wait(p, kind)
        for kind in range(4):
            spread_copy(p, kind).wait_send()
        return carry

    lax.fori_loop(0, 7, spread_end, 0)

    def rows_wait(n, carry):
        g = lax.rem(place + n, places)
        for h in range(2):
            remote(
                att_out.at[h, g], att_in.at[g, h], att_sent.at[h, g], att_came.at[h, g], to_head(g)
            ).wait()
        return carry

    lax.fori_loop(1, places, rows_wait, 0)

    width = 256

    def project(c, carry):
        cols = pl.ds(aligned(c, width), width)
        acc = None
        for n in range(places):
            g = lax.rem(place + n, places)
            left = jnp.concatenate([att_in[g, 0], att_in[g, 1]], 1)
            right = (w_own[:, :, cols] if n == 0 else w_all[g, :, :, cols]).reshape(
                2 * HEAD_DIM, width
            )
            term = lax.dot_general(left, right, NN, preferred_element_type=F32)
            acc = term if acc is None else acc + term
        out_ref[:, cols] = acc.astype(BF16)
        return carry

    lax.fori_loop(0, out_ref.shape[1] // width, project, 0)

    def sent_wait(n, carry):
        for source in range(2):
            @pl.when(helped[source])
            def _():
                query_copy(n, source).wait_send()

            @pl.when(asked[source])
            def _():
                answer_copy(n, source).wait_send()

        return carry

    lax.fori_loop(0, groups, sent_wait, 0)


def planned(near, shards, places, pattern, q, k, v, w):
    rows = q.shape[0]
    flat = lambda array: array.reshape(rows * 2, HEAD_DIM)
    tiles = rows // TILE
    pairs = tiles // 2
    answers = 4 * pairs
    dma = pltpu.SemaphoreType.DMA
    vm = pltpu.VMEM
    return pl.pallas_call(
        functools.partial(whole_kernel, near, shards, places),
        in_specs=[pl.BlockSpec(memory_space=pl.ANY)] + [WHOLE] * 4,
        out_specs=WHOLE,
        out_shape=jax.ShapeDtypeStruct((rows // places, w.shape[2]), BF16),
        scratch_shapes=[
            pltpu.SMEM((3, 2, rows // BLOCK, pattern.shape[2]), jnp.int32),
            vm((2, PAIR, HEAD_DIM), F32),
            vm((2, rows, HEAD_DIM), BF16),
            vm((2, HEAD_DIM, rows), BF16),
            vm((6, rows, HEAD_DIM), BF16),
            vm((2 * pairs + answers, OUT_ROWS, PAIR), BF16),
            vm((answers, OUT_ROWS, PAIR), BF16),
            vm((rows, TILE), F32),
            vm((rows, TILE), F32),
            vm((TILE, TILE), F32),
            vm((TILE, TILE), F32),
            vm((8, TILE), F32),
            vm((8, TILE), F32),
            vm((HEAD_DIM, TILE), F32),
            vm((8, TILE), F32),
            vm((2, places, TILE, HEAD_DIM), BF16),
            vm((places, 2, TILE, HEAD_DIM), BF16),
            vm((places, 2, HEAD_DIM, w.shape[2]), BF16),
            dma((answers,)), dma((answers,)), dma((answers,)), dma((answers,)),
            dma((2, places)), dma((2, places)), dma((9,)), dma((9,)), dma((28,)), dma((28,)), dma((3,)),
        ],
        compiler_params=pltpu.CompilerParams(
            collective_id=near, has_side_effects=True, vmem_limit_bytes=VMEM_LIMIT
        ),
        name=f"whole_{near}",
    )(pattern, flat(q), flat(k), flat(v), w)


def per_device(query_states, key_states, value_states, block_pattern, helper_distances, out_weight):
    shards, places = lax.axis_size("ctx"), lax.axis_size("head")
    near = jnp.minimum(helper_distances[0], helper_distances[1])
    branches = [functools.partial(planned, r, shards, places) for r in range(1, FAR)]
    return lax.switch(
        near - 1, branches, block_pattern, query_states, key_states, value_states, out_weight
    )


def solution(mesh):
    placed = (
        P("ctx", "head", None),
        P("ctx", "head", None),
        P("ctx", "head", None),
        P("head", None, None),
        P(),
        P("head", None, None),
    )
    return jax.shard_map(
        per_device, mesh=mesh, in_specs=placed, out_specs=P(("ctx", "head"), None), check_vma=False
    )
```

time: 155 us -> 113 us (0.73)
  Pallas kernels: 144 us -> 106 us
  local copies, waits for them, and re-layouts: 7.21 us -> 2.63 us
    pallas_call x1, Pallas kernels: 144 us -> 106 us  [planned(): pl.pallas_call(functools.partial(whole_kernel, near, shards, places), in_...]
    unnamed x5 -> x1, local copies, waits for them, and re-layouts: 4.44 us -> 1.32 us
where the time goes in v2:
time: 113 us; the launch traced here: 110 us
  Pallas kernels  106 us (94%)
  local copies, waits for them, and re-layouts  2.63 us (2%)
  between operations  1.3 us (1%)
    pallas_call x1, Pallas kernels, planned(): pl.pallas_call(functools.partial(whole_kernel, near, shards, places), in_...  106 us

profile of v2, /device:TPU:23, one launch (start us, length us, event | category | flops | bytes accessed | tf_op | source)
XLA Modules:
  0.0 110.3 jit_solution(17361637291323966364)
XLA Ops:
  0.0 1.3 %fusion = (s32[1]{0:T(128)}, s32[1]{0:T(128)}) fusion(s32[2]{0:T(128)} %param.17), kind=kLoop, calls=%fused_computation | loop fusion | bytes 16 | tf_op jit(solution)/shard_map/slice | solution.py:551
  2.6 106.4 %conditional.1 = (bf16[256,4096]{1,0:T(8,128)(2,1)S(1)}) conditional(s32[]{:T(128)} %bitcast.21, (bf16[2048,2,128]{2,1,0:T(2,128)(2,1)}, bf16[2048,2,128]{2,1,0:T(2,128)(2,1)}, bf16[2048,2,128]{2,1,0:T(2,128)(2,1)}, s32[2,256,256]{2,1,0:T(8,128)}, bf16[2,128,4096]{2,1,0:T(8,128)(2,1)}) %tuple.26, ...), branch_computations={%region_0.0_spmd, %region_1.0_spmd, %region_2.0_spmd, %region_3.0_... | conditional | bytes 8 | solution.py:553
  2.9 105.8 %whole_6.1 = bf16[256,4096]{1,0:T(8,128)(2,1)S(1)} custom-call(s32[2,256,256]{2,1,0:T(8,128)} %get-tuple-element.108.pattern_all, bf16[4096,128]{1,0:T(8,128)(2,1)} %bitcast.27, bf16[4096,128]{1,0:T(8,128)(2,1)} %bitcast.34, bf16[4096,128]{1,0:T(8,128)(2,1)} %bitcast.41, bf16[2,128,4096]{2,1,0:T(8,128)(2,1)} %get-tuple-element.112.w_own), custom_call_target="tpu_custom_call" | custom-call | tf_op jit(solution)/shard_map/cond/branch_5_fun/whole_6/pallas_call | solution.py:515
  109.0 1.3 %copy.22 = bf16[256,4096]{1,0:T(8,128)(2,1)} copy(bf16[256,4096]{1,0:T(8,128)(2,1)S(1)} %get-tuple-element.118) | data formatting | bytes 4194304

commit v3 on v2

--- a/solution.py
+++ b/solution.py
@@ -25,7 +25,7 @@
 WHOLE = pl.BlockSpec(memory_space=pltpu.VMEM)
 VMEM_LIMIT = 60 << 20
 LAG = 3
-EVENTS = (10, 13, 16, 23)
+EVENTS = (8, 10, 13, 18)
 
 
 def three_parts(x):
@@ -41,8 +41,8 @@
 
 def whole_kernel(
     near, shards, places,
-    pattern_all, q_raw, k_raw, v_raw, w_own, out_ref,
-    pattern, wide, keys, values, queries, made, came, s_a, s_b, diag_a, diag_b, peak_ref,
+    pattern_all, q_raw, k_hbm, v_hbm, w_hbm, out_ref,
+    pattern, k_raw, v_raw, w_own, loaded, wide, keys, values, queries, made, came, s_a, s_b, diag_a, diag_b, peak_ref,
     peak_start, acc_start, total_start, att_out, att_in, w_all,
     q_sent, q_came, made_sent, made_came, att_sent, att_came, w_sent, w_came, spread_sent, spread_came, bits_came,
 ):
@@ -89,6 +89,12 @@
             bits_came.at[source],
         )
 
+    loads = [
+        pltpu.make_async_copy(src, dst, loaded.at[n])
+        for n, (src, dst) in enumerate(((w_hbm, w_own), (k_hbm, k_raw), (v_hbm, v_raw)))
+    ]
+    for load in loads:
+        load.start()
     for source in range(3):
         bits_copy(source).start()
 
@@ -213,6 +219,7 @@
         lax.fori_loop(first, last + 1, body, 0)
 
     lax.fori_loop(0, pairs, send_queries, 0)
+    loads[0].wait()
     for n in range(3):
         forward(n).start()
     lax.fori_loop(pairs, groups, send_queries, 0)
@@ -226,6 +233,8 @@
             values[h, :, to] = wide[1, pl.ds(h, TILE, stride=2), :].T.astype(BF16)
         return carry
 
+    for load in loads[1:]:
+        load.wait()
     lax.fori_loop(0, tiles, split_kv, 0)
 
     def where_of(t):
@@ -444,11 +453,14 @@
         combine(n)
         return carry
 
-    lax.fori_loop(groups - lag, groups + 1, merge_rest, 0)
     for n in (7, 8):
         arrived(n)
     spread(6, 6)
-    settle(3, 6)
+    settle(3, 3)
+    lax.fori_loop(groups - lag, groups - 1, merge_rest, 0)
+    settle(4, 5)
+    lax.fori_loop(groups - 1, groups + 1, merge_rest, 0)
+    settle(6, 6)
     for n in range(9):
         forward(n).wait_send()
 
@@ -514,11 +526,15 @@
     vm = pltpu.VMEM
     return pl.pallas_call(
         functools.partial(whole_kernel, near, shards, places),
-        in_specs=[pl.BlockSpec(memory_space=pl.ANY)] + [WHOLE] * 4,
+        in_specs=[pl.BlockSpec(memory_space=pl.ANY), WHOLE] + [pl.BlockSpec(memory_space=pl.ANY)] * 3,
         out_specs=WHOLE,
         out_shape=jax.ShapeDtypeStruct((rows // places, w.shape[2]), BF16),
         scratch_shapes=[
             pltpu.SMEM((3, 2, rows // BLOCK, pattern.shape[2]), jnp.int32),
+            vm((2 * rows, HEAD_DIM), BF16),
+            vm((2 * rows, HEAD_DIM), BF16),
+            vm(w.shape, BF16),
+            dma((3,)),
             vm((2, PAIR, HEAD_DIM), F32),
             vm((2, rows, HEAD_DIM), BF16),
             vm((2, HEAD_DIM, rows), BF16),

time: 113 us -> 109 us (0.965); the launches traced: 110 us -> 109 us
  Pallas kernels: 106 us -> 104 us
    pallas_call x1, Pallas kernels: 106 us -> 104 us  [planned(): pl.pallas_call(functools.partial(whole_kernel, near, shards, places), in_...]
where the time goes in v3:
time: 109 us
  Pallas kernels  104 us (95%)
  local copies, waits for them, and re-layouts  2.63 us (2%)
  between operations  1.3 us (1%)
    pallas_call x1, Pallas kernels, planned(): pl.pallas_call(functools.partial(whole_kernel, near, shards, places), in_...  104 us

profile of v3, /device:TPU:23, one launch (start us, length us, event | category | flops | bytes accessed | tf_op | source)
XLA Modules:
  0.0 108.7 jit_solution(10631017226243279630)
XLA Ops:
  0.0 1.3 %fusion = (s32[1]{0:T(128)}, s32[1]{0:T(128)}) fusion(s32[2]{0:T(128)} %param.17), kind=kLoop, calls=%fused_computation | loop fusion | bytes 16 | tf_op jit(solution)/shard_map/slice | solution.py:567
  2.6 104.7 %conditional.1 = (bf16[256,4096]{1,0:T(8,128)(2,1)S(1)}) conditional(s32[]{:T(128)} %bitcast.21, (bf16[2048,2,128]{2,1,0:T(2,128)(2,1)}, bf16[2048,2,128]{2,1,0:T(2,128)(2,1)}, bf16[2048,2,128]{2,1,0:T(2,128)(2,1)}, s32[2,256,256]{2,1,0:T(8,128)}, bf16[2,128,4096]{2,1,0:T(8,128)(2,1)}) %tuple.26, ...), branch_computations={%region_0.0_spmd, %region_1.0_spmd, %region_2.0_spmd, %region_3.0_... | conditional | bytes 8 | solution.py:569
  2.6 104.1 %whole_3.1 = bf16[256,4096]{1,0:T(8,128)(2,1)S(1)} custom-call(s32[2,256,256]{2,1,0:T(8,128)} %get-tuple-element.93.pattern_all, bf16[4096,128]{1,0:T(8,128)(2,1)} %bitcast.24, bf16[4096,128]{1,0:T(8,128)(2,1)} %bitcast.31, bf16[4096,128]{1,0:T(8,128)(2,1)} %bitcast.38, bf16[2,128,4096]{2,1,0:T(8,128)(2,1)} %get-tuple-element.97.w_hbm), custom_call_target="tpu_custom_call" | custom-call | tf_op jit(solution)/shard_map/cond/branch_2_fun/whole_3/pallas_call | solution.py:527
  107.3 1.3 %copy.22 = bf16[256,4096]{1,0:T(8,128)(2,1)} copy(bf16[256,4096]{1,0:T(8,128)(2,1)S(1)} %get-tuple-element.118) | data formatting | bytes 4194304
